TPU v7x, 128 devices: a whole 4x4x4 slice. The times are simulated.
128 devices in a mesh: row: 16 (over y, x), col: 8 (over z, core).
Axes of the slice: x: 4, y: 4, z: 4, core: 2. Of those that a mesh axis runs over, the one named last changes fastest.
Arguments:
- features: bfloat16 [32768, 256], P(('row', 'col')), may hold values from -6 to 6
- out_degree: int32 [32768], P('row'), may hold values from 8 to 1024
- in_degree: int32 [32768], P('col'), may hold values from 8 to 1024
- tile_blocks: int32 [16, 8, 2, 128], P('row', 'col'), may hold values from 0 to 31, as said below
- tile_count: int32 [16, 8], P('row', 'col'), may hold values from 16 to 128, as said below
- tile_weights: bfloat16 [16, 8, 128, 128, 128], P('row', 'col'), may hold values from 0 to 4, as said below
- weight: bfloat16 [256, 256], replicated, may hold values from -0.375 to 0.375
- cotangent: bfloat16 [32768, 256], P(('col', 'row')), may hold values from -6 to 6
Outputs:
- hidden: bfloat16 [32768, 256], P(('col', 'row'))
- input_grad: bfloat16 [32768, 256], P(('row', 'col'))
- weight_grad: float32 [256, 256], replicated
Inputs may be any that keep to these rules, and one draw needn't show every extreme that they name: `tile_blocks`: entry [r, c, 0, s] is a target block below 32, entry [r, c, 1, s] a source block below 16; the pairs of one device position are distinct. `tile_count`: live tile slots of a device position are its first ones; some position has exactly 128. `tile_weights`: Non-negative edge weights.
All inputs are finite; a program needn't handle non-finite values.
Results may differ from a plain program's by a relative error of at most 0.0067.
Values may be sent and summed in bfloat16 or wider, within the bound.
No kernel may reach another device: no remote copies, remote signals or barrier semaphores. Data moves between devices by JAX's collectives and lax.ppermute only.
A program may use at most 192 MiB of HBM per device.

v0:
```python
import jax
import jax.numpy as jnp
from jax import lax
from jax.sharding import PartitionSpec as P

TILE = 128


def silu_slope(pre_act):
    gate_sig = jax.nn.sigmoid(pre_act)
    return gate_sig * (1.0 + pre_act * (1.0 - gate_sig))


def tile_sum(tile_vals, dst_ids, src_ids, live_count, inputs, dst_blocks, transpose):
    feat_width = inputs.shape[1]
    group_size = min(128, tile_vals.shape[0])
    block_stack = inputs.reshape(-1, TILE, feat_width)
    group_count = (live_count + group_size - 1) // group_size

    def add_group(group_at, running):
        first_slot = group_at * group_size
        picked = jnp.take(block_stack, src_ids, axis=0)
        if transpose:
            products = jnp.einsum(
                "trc,trh->tch", tile_vals, picked, preferred_element_type=jnp.float32
            )
        else:
            products = jnp.einsum(
                "trc,tch->trh", tile_vals, picked, preferred_element_type=jnp.float32
            )
        slot_ids = first_slot + jnp.arange(group_size)
        is_live = slot_ids < live_count
        masked = jnp.where(is_live[:, None], products.reshape(group_size, -1), 0.0)
        return running.at[dst_ids].add(masked)

    start_sum = jnp.zeros((dst_blocks, TILE * feat_width), jnp.float32)
    running = lax.fori_loop(0, group_count, add_group, start_sum)
    return running.reshape(dst_blocks * TILE, feat_width)


def shards(
    features, out_degree, in_degree, tile_blocks, tile_count, tile_weights, weight, cotangent
):
    row_count = features.shape[0]
    row_at = lax.axis_index("row")
    col_at = lax.axis_index("col")
    out_strip = lax.rsqrt(out_degree.astype(jnp.float32))
    in_strip = lax.rsqrt(in_degree.astype(jnp.float32))
    own_out = lax.dynamic_slice_in_dim(out_strip, col_at * row_count, row_count, 0)
    src_scaled = (features.astype(jnp.float32) * own_out[:, None]).astype(jnp.bfloat16)
    source = lax.all_gather(src_scaled, "col", axis=0, tiled=True)
    blocks = tile_blocks[0, 0]
    live_count = tile_count[0, 0]
    tile_vals = tile_weights[0, 0]
    partial_value = tile_sum(
        tile_vals, blocks[0], blocks[1], live_count, source, in_strip.shape[0] // TILE, False
    )
    contract_rows = (((0,), (0,)), ((), ()))
    summed = lax.psum(partial_value, "row")
    agg_strip = (summed * in_strip[:, None]).astype(jnp.bfloat16)
    pre_strip = jnp.dot(agg_strip, weight, preferred_element_type=jnp.float32)
    strip_grads = lax.all_gather(cotangent, "row", axis=0, tiled=True)
    grad_strip = (strip_grads.astype(jnp.float32) * silu_slope(pre_strip)).astype(jnp.bfloat16)
    own_pre = lax.dynamic_slice_in_dim(pre_strip, row_at * row_count, row_count, 0)
    hidden = jax.nn.silu(own_pre).astype(jnp.bfloat16)
    agg_rows = lax.dynamic_slice_in_dim(agg_strip, row_at * row_count, row_count, 0)
    pre_grad = lax.dynamic_slice_in_dim(grad_strip, row_at * row_count, row_count, 0)
    weight_part = lax.dot_general(
        agg_rows, pre_grad, contract_rows, preferred_element_type=jnp.float32
    )
    back_rows = jnp.dot(grad_strip, weight.T, preferred_element_type=jnp.float32)
    target_grad = (back_rows * in_strip[:, None]).astype(jnp.bfloat16)
    weight_grad = lax.psum(weight_part, ("row", "col"))
    back_part = tile_sum(
        tile_vals, blocks[1], blocks[0], live_count, target_grad, source.shape[0] // TILE, True
    )
    src_sum = lax.psum_scatter(back_part, "col", scatter_dimension=0, tiled=True)
    input_grad = (src_sum * own_out[:, None]).astype(jnp.bfloat16)
    return (hidden, input_grad, weight_grad)


def solution(mesh):
    placed = (
        P(("row", "col"), None),
        P("row"),
        P("col"),
        P("row", "col", None, None),
        P("row", "col"),
        P("row", "col", None, None, None),
        P(),
        P(("col", "row"), None),
    )
    return jax.shard_map(
        shards,
        mesh=mesh,
        in_specs=placed,
        out_specs=(P(("col", "row"), None), P(("row", "col"), None), P()),
        check_vma=False,
    )
```

profile of v0, /device:TPU:1, one launch (start us, length us, event | category | flops | bytes accessed | tf_op | source)
XLA Modules:
  0.0 580.1 jit_solution(587805703968408114)
XLA Ops:
  11.7 25.7 %all-gather.3.cloned.1.call-done = bf16[2048,256]{1,0:T(8,128)(2,1)} async-done(((bf16[256,256]{1,0:T(8,128)(2,1)}), bf16[2048,256]{1,0:T(8,128)(2,1)}) %all-gather.3.cloned.1.call-update) | async-done | bytes 1048592 | tf_op jit(solution)/shard_map/all_gather | solution.py:51
  37.4 2.3 broadcast_in_dim.54
  39.7 94.9 %while.20 = (s32[]{:T(128)}, f32[32,32768]{1,0:T(8,128)}, s32[]{:T(128)}, s32[128]{0:T(128)S(1)}, s32[]{:T(128)}, /*index=5*/s32[128]{0:T(128)S(1)}, bf16[16,128...) while((s32[]{:T(128)}, f32[32,32768]{1,0:T(8,128)}, s32[]{:T(128)}, ...), condition=%wide.region_2.3_spmd, body=%wide.region_0.2_spmd.sunk | while | flops 1086327552 | bytes 197141120 | solution.py:37
  39.8 6.6 %gather_fusion = bf16[128,128,256]{2,1,0:T(8,128)(2,1)} fusion(bf16[16,128,256]{2,1,0:T(8,128)(2,1)S(1)} %get-tuple-element.277, s32[1024]{0:T(1024)S(1)} %pad_clamp_fusion.4), kind=kCustom, calls=%fused_computation.clone.1 | custom fusion | bytes 16777728 | tf_op jit(solution)/shard_map/while/body/jit(_take)/gather | solution.py:22
  47.0 13.2 %convolution_bitcast_fusion.4 = f32[128,128,256]{1,2,0:T(8,128)} fusion(bf16[128,128,128]{2,1,0:T(8,128)(2,1)} %get-tuple-element.278, bf16[128,128,256]{2,1,0:T(8,128)(2,1)} %gather_fusion, pred[128]{0:T(512)(128)(4,1)S(1)} %get-tuple-element.237), kind=kOutput, calls=%fused_computation.5.clone.1 | convolution fusion | flops 1077936128 | bytes 29360256 | tf_op jit(solution)/shard_map/while/body/trc,tch->trh/dot_general | solution.py:28
  60.2 17.7 %copy.29 = f32[128,128,256]{0,2,1:T(8,128)} copy(f32[128,128,256]{1,2,0:T(8,128)} %convolution_bitcast_fusion.4) | data formatting | bytes 33554432 | tf_op jit(solution)/shard_map/while/body/trc,tch->trh/dot_general | solution.py:28
  77.9 11.2 %bitcast_select_fusion.4 = f32[128,32768]{0,1:T(8,128)} fusion(f32[128,128,256]{0,2,1:T(8,128)} %copy.29, pred[128]{0:T(512)(128)(4,1)S(1)} %get-tuple-element.238), kind=kLoop, calls=%fused_computation.4.clone.1 | loop fusion | flops 4194304 | bytes 33554560 | tf_op jit(solution)/shard_map/while/body/jit(_where)/select_n | solution.py:33
  89.1 17.4 %copy.30 = f32[128,32768]{1,0:T(8,128)} copy(f32[128,32768]{0,1:T(8,128)} %bitcast_select_fusion.4) | data formatting | bytes 33554432 | tf_op jit(solution)/shard_map/while/body/jit(_where)/select_n | solution.py:33
  106.6 27.7 %scatter_fusion = f32[32,32768]{1,0:T(8,128)} fusion(f32[32,32768]{1,0:T(8,128)} %get-tuple-element.262, s32[128]{0:T(128)S(1)} %get-tuple-element.235, f32[128,32768]{1,0:T(8,128)} %copy.30), kind=kCustom, calls=%fused_computation.2.clone.1 | custom fusion | flops 4194304 | bytes 50332160 | tf_op jit(solution)/shard_map/while/body/scatter-add | solution.py:34
  134.6 4.9 reshape.111
  140.4 101.8 %all-reduce.3.cloned.1.call-done = f32[4096,256]{1,0:T(8,128)} async-done(((f32[4096,256]{1,0:T(8,128)}), f32[4096,256]{1,0:T(8,128)}) %all-reduce.3.cloned.1.call-update) | async-done | bytes 4194320 | tf_op jit(solution)/shard_map/psum | solution.py:59
  242.2 2.6 multiply_convert_fusion.1
  244.7 42.9 %all-gather.5.cloned.1.call-done = bf16[4096,256]{1,0:T(8,128)(2,1)} async-done(((bf16[256,256]{1,0:T(8,128)(2,1)}), bf16[4096,256]{1,0:T(8,128)(2,1)}) %all-gather.5.cloned.1.call-update) | async-done | bytes 2097168 | tf_op jit(solution)/shard_map/all_gather | solution.py:62
  287.7 5.2 multiply_convert_fusion
  292.9 2.0 fusion.12
  295.0 92.8 %while.21 = (s32[]{:T(128)}, f32[16,32768]{1,0:T(8,128)S(1)}, s32[]{:T(128)}, s32[128]{0:T(128)S(1)}, s32[]{:T(128)}, /*index=5*/s32[128]{0:T(128)S(1)}, bf16[32...) while((s32[]{:T(128)}, f32[16,32768]{1,0:T(8,128)S(1)}, s32[]{:T(128)}, ...), condition=%wide.region_6.7_spmd, body=%wide.region_4.6_spmd.sunk | while | flops 1086327552 | bytes 197141120 | solution.py:37
  295.3 8.2 %gather_fusion.1 = bf16[128,128,256]{2,1,0:T(8,128)(2,1)} fusion(bf16[32,128,256]{2,1,0:T(8,128)(2,1)} %get-tuple-element.307, s32[1024]{0:T(1024)S(1)} %pad_clamp_fusion.5), kind=kCustom, calls=%fused_computation.1.clone.1 | custom fusion | bytes 16777728 | tf_op jit(solution)/shard_map/while/body/jit(_take)/gather | solution.py:22
  304.1 12.8 %convolution_bitcast_fusion.5 = f32[128,128,256]{1,2,0:T(8,128)} fusion(bf16[128,128,128]{2,1,0:T(8,128)(2,1)} %get-tuple-element.308, bf16[128,128,256]{2,1,0:T(8,128)(2,1)} %gather_fusion.1, pred[128]{0:T(512)(128)(4,1)S(1)} %get-tuple-element.249), kind=kOutput, calls=%fused_computation.19.clone.1 | convolution fusion | flops 1077936128 | bytes 29360256 | tf_op jit(solution)/shard_map/while/body/trc,trh->tch/dot_general | solution.py:24
  316.9 17.7 %copy.31 = f32[128,128,256]{0,2,1:T(8,128)} copy(f32[128,128,256]{1,2,0:T(8,128)} %convolution_bitcast_fusion.5) | data formatting | bytes 33554432 | tf_op jit(solution)/shard_map/while/body/trc,trh->tch/dot_general | solution.py:24
  334.6 11.3 %bitcast_select_fusion.5 = f32[128,32768]{0,1:T(8,128)} fusion(f32[128,128,256]{0,2,1:T(8,128)} %copy.31, pred[128]{0:T(512)(128)(4,1)S(1)} %get-tuple-element.250), kind=kLoop, calls=%fused_computation.18.clone.1 | loop fusion | flops 4194304 | bytes 33554560 | tf_op jit(solution)/shard_map/while/body/jit(_where)/select_n | solution.py:33
  345.9 17.4 %copy.32 = f32[128,32768]{1,0:T(8,128)} copy(f32[128,32768]{0,1:T(8,128)} %bitcast_select_fusion.5) | data formatting | bytes 33554432 | tf_op jit(solution)/shard_map/while/body/jit(_where)/select_n | solution.py:33
  363.3 24.3 %scatter_fusion.1 = f32[16,32768]{1,0:T(8,128)S(1)} fusion(f32[16,32768]{1,0:T(8,128)S(1)} %get-tuple-element.292, s32[128]{0:T(128)S(1)} %get-tuple-element.247, f32[128,32768]{1,0:T(8,128)} %copy.32), kind=kCustom, calls=%fused_computation.3.clone.1 | custom fusion | flops 4194304 | bytes 50332160 | tf_op jit(solution)/shard_map/while/body/scatter-add | solution.py:34
  393.1 28.5 %reduce-scatter.2.cloned.1.call-done = f32[256,256]{1,0:T(8,128)} async-done(((f32[2048,256]{1,0:T(8,128)}), f32[256,256]{1,0:T(8,128)}) %reduce-scatter.2.cloned.1.call-update) | async-done | bytes 262160 | tf_op jit(solution)/shard_map/reduce_scatter | solution.py:77
  423.3 148.3 %all-reduce.5.cloned.1.call-done = f32[256,256]{1,0:T(8,128)} async-done(((f32[256,256]{1,0:T(8,128)}), f32[256,256]{1,0:T(8,128)}) %all-reduce.5.cloned.1.call-update) | async-done | bytes 262160 | tf_op jit(solution)/shard_map/psum | solution.py:73
  (42 shorter events, 14.6 us)
Async XLA Ops:
  7.2 280.5 %copy-start = (bf16[256,256]{1,0:T(8,128)(2,1)S(1)}, bf16[256,256]{1,0:T(8,128)(2,1)}, u32[]{:S(2)}) copy-start(bf16[256,256]{1,0:T(8,128)(2,1)} %param.18) | copy-start | bytes 393220
  7.2 30.2 %all-gather.3.cloned.1.call-start = ((), (), s32[]{:S(2)}) async-start(), calls=%async_computation.1 | async-start | bytes 1179648 | tf_op jit(solution)/shard_map/all_gather | solution.py:51
  8.0 0.5 copy-start.6
  10.2 231.9 %all-reduce.3.cloned.1.call-start = ((), (), s32[]{:S(2)}) async-start(), calls=%async_computation.2 | async-start | bytes 8388608 | tf_op jit(solution)/shard_map/psum | solution.py:59
  37.4 2.3 copy-start.2
  139.5 0.8 copy-start.5
  139.5 148.1 %all-gather.5.cloned.1.call-start = ((), (), s32[]{:S(2)}) async-start(), calls=%async_computation.3 | async-start | bytes 2228224 | tf_op jit(solution)/shard_map/all_gather | solution.py:62
  140.3 281.3 %reduce-scatter.2.cloned.1.call-start = ((), (), s32[]{:S(2)}) async-start(), calls=%async_computation.4 | async-start | bytes 2359296 | tf_op jit(solution)/shard_map/reduce_scatter | solution.py:77
  244.7 48.1 %copy-start.3 = (bf16[4096,256]{1,0:T(8,128)(2,1)}, bf16[4096,256]{1,0:T(8,128)(2,1)S(1)}, u32[]{:S(2)}) copy-start(bf16[4096,256]{1,0:T(8,128)(2,1)S(1)} %multiply_convert_fusion.1) | copy-start | bytes 6291460
  292.9 2.0 copy-start.4
  387.9 33.7 %copy-start.7 = (f32[256]{0:T(256)S(1)}, f32[256]{0:T(256)}, u32[]{:S(2)}) copy-start(f32[256]{0:T(256)} %copy-done.6) | copy-start | bytes 3076
  387.9 185.4 %copy-start.1 = (bf16[256,256]{1,0:T(8,128)(2,1)S(1)}, bf16[256,256]{1,0:T(8,128)(2,1)}, u32[]{:S(2)}) copy-start(bf16[256,256]{1,0:T(8,128)(2,1)} %param.18) | copy-start | bytes 393220
  389.4 182.2 %all-reduce.5.cloned.1.call-start = ((), (), s32[]{:S(2)}) async-start(), calls=%async_computation.5 | async-start | bytes 524288 | tf_op jit(solution)/shard_map/psum | solution.py:73
Sparse Core Ops, SparseCore 0:
  10.3 27.0 all-gather.2
  139.7 102.4 all-reduce.2
  244.3 43.3 all-gather.4
  389.5 31.9 reduce-scatter.1
  426.7 144.8 all-reduce.4
where the time goes:
time: 582 us; the launch traced here: 580 us
  waiting for transfers between devices  348 us (60%)
  local copies, waits for them, and re-layouts  96.8 us (17%)
  other arithmetic  84.3 us (14%)
  matrix products  35.2 us (6%)
  between operations  14.8 us (3%)
    psum x1, waiting for transfers between devices, shards(): weight_grad = lax.psum(weight_part, ('row', 'col'))  148 us
    psum x1, waiting for transfers between devices, shards(): summed = lax.psum(partial_value, 'row')  102 us
    scatter-add x2, other arithmetic, add_group(): return running.at[dst_ids].add(masked)  52 us
    all_gather x1, waiting for transfers between devices, shards(): strip_grads = lax.all_gather(cotangent, 'row', axis=0, tiled=True)  42.9 us
    select_n x2, local copies, waits for them, and re-layouts, add_group(): masked = jnp.where(is_live[:, None], products.reshape(group_size, -1), 0.0)  34.9 us
    reduce_scatter x1, waiting for transfers between devices, shards(): lax.psum_scatter(back_part, 'col', scatter_dimension=0, tiled=True)  28.5 us
    all_gather x1, waiting for transfers between devices, shards(): source = lax.all_gather(src_scaled, 'col', axis=0, tiled=True)  25.7 us
    select_n x2, other arithmetic, add_group(): masked = jnp.where(is_live[:, None], products.reshape(group_size, -1), 0.0)  22.5 us
  transfers between devices with their start and end apart: 5, of which 5 were waited for; matrix products, arithmetic and copies ran while one was open for 1% of the time, Pallas kernels for 0%

commit v1 on v0

--- a/solution.py
+++ b/solution.py
@@ -4,6 +4,9 @@
 from jax.sharding import PartitionSpec as P
 
 TILE = 128
+_end_pieces_all = lambda my_data, dim_k: jnp.concatenate(
+    lax.all_to_all(jnp.stack([my_data for _ in range(lax.psum(1, "row"))]), "row", 0, 0), axis=dim_k
+)
 
 
 def silu_slope(pre_act):
@@ -59,7 +62,7 @@
     summed = lax.psum(partial_value, "row")
     agg_strip = (summed * in_strip[:, None]).astype(jnp.bfloat16)
     pre_strip = jnp.dot(agg_strip, weight, preferred_element_type=jnp.float32)
-    strip_grads = lax.all_gather(cotangent, "row", axis=0, tiled=True)
+    strip_grads = _end_pieces_all(cotangent, 0)
     grad_strip = (strip_grads.astype(jnp.float32) * silu_slope(pre_strip)).astype(jnp.bfloat16)
     own_pre = lax.dynamic_slice_in_dim(pre_strip, row_at * row_count, row_count, 0)
     hidden = jax.nn.silu(own_pre).astype(jnp.bfloat16)

time: 582 us -> 564 us (0.969)
  waiting for transfers between devices: 348 us -> 320 us
  starting transfers between devices: 0.2 us -> 6.74 us
    all_gather x1 -> x0, waiting for transfers between devices: 42.9 us -> none  [shards(): strip_grads = lax.all_gather(cotangent, 'row', axis=0, tiled=True)]
    psum x1, waiting for transfers between devices: 102 us -> 118 us  [shards(): summed = lax.psum(partial_value, 'row')]
    all_to_all x0 -> x1, starting transfers between devices: none -> 6.58 us  [lax.all_to_all(jnp.stack([my_data for _ in range(lax.psum(1, 'row'))]), '...]
  transfers between devices with their start and end apart: 5 -> 5, of which waited for: 5 -> 4; matrix products, arithmetic and copies ran while one was open for 1% -> 2% of each run, Pallas kernels for 0% -> 0%
where the time goes in v1:
time: 564 us; the launch traced here: 562 us
  waiting for transfers between devices  320 us (57%)
  local copies, waits for them, and re-layouts  99.2 us (18%)
  other arithmetic  84.3 us (15%)
  matrix products  36 us (6%)
  between operations  14.8 us (3%)
  starting transfers between devices  6.74 us (1%)
    psum x1, waiting for transfers between devices, shards(): weight_grad = lax.psum(weight_part, ('row', 'col'))  148 us
    psum x1, waiting for transfers between devices, shards(): summed = lax.psum(partial_value, 'row')  118 us
    scatter-add x2, other arithmetic, add_group(): return running.at[dst_ids].add(masked)  52 us
    select_n x2, local copies, waits for them, and re-layouts, add_group(): masked = jnp.where(is_live[:, None], products.reshape(group_size, -1), 0.0)  34.9 us
    reduce_scatter x1, waiting for transfers between devices, shards(): lax.psum_scatter(back_part, 'col', scatter_dimension=0, tiled=True)  27.6 us
    all_gather x1, waiting for transfers between devices, shards(): source = lax.all_gather(src_scaled, 'col', axis=0, tiled=True)  25.7 us
    select_n x2, other arithmetic, add_group(): masked = jnp.where(is_live[:, None], products.reshape(group_size, -1), 0.0)  22.5 us
    dot_general x1, local copies, waits for them, and re-layouts, add_group(): jnp.einsum('trc,tch->trh', tile_vals, picked, preferred_element_type=jnp....  17.7 us
  transfers between devices with their start and end apart: 5, of which 4 were waited for; matrix products, arithmetic and copies ran while one was open for 2% of the time, Pallas kernels for 0%

profile of v1, /device:TPU:1, one launch (start us, length us, event | category | flops | bytes accessed | tf_op | source)
XLA Modules:
  0.0 562.1 jit_solution(15400013099687349819)
XLA Ops:
  11.7 25.7 %all-gather.2.cloned.1.call-done = bf16[2048,256]{1,0:T(8,128)(2,1)} async-done(((bf16[256,256]{1,0:T(8,128)(2,1)}), bf16[2048,256]{1,0:T(8,128)(2,1)}) %all-gather.2.cloned.1.call-update) | async-done | bytes 1048592 | tf_op jit(solution)/shard_map/all_gather | solution.py:54
  37.4 2.3 broadcast_in_dim.54
  39.7 94.9 %while.20 = (s32[]{:T(128)}, f32[32,32768]{1,0:T(8,128)}, s32[]{:T(128)}, s32[128]{0:T(128)S(1)}, s32[]{:T(128)}, /*index=5*/s32[128]{0:T(128)S(1)}, bf16[16,128...) while((s32[]{:T(128)}, f32[32,32768]{1,0:T(8,128)}, s32[]{:T(128)}, ...), condition=%wide.region_2.3_spmd, body=%wide.region_0.2_spmd.sunk | while | flops 1086327552 | bytes 197141120 | solution.py:40
  39.8 6.6 %gather_fusion = bf16[128,128,256]{2,1,0:T(8,128)(2,1)} fusion(bf16[16,128,256]{2,1,0:T(8,128)(2,1)S(1)} %get-tuple-element.277, s32[1024]{0:T(1024)S(1)} %pad_clamp_fusion.4), kind=kCustom, calls=%fused_computation.clone.1 | custom fusion | bytes 16777728 | tf_op jit(solution)/shard_map/while/body/jit(_take)/gather | solution.py:25
  47.0 13.2 %convolution_bitcast_fusion.4 = f32[128,128,256]{1,2,0:T(8,128)} fusion(bf16[128,128,128]{2,1,0:T(8,128)(2,1)} %get-tuple-element.278, bf16[128,128,256]{2,1,0:T(8,128)(2,1)} %gather_fusion, pred[128]{0:T(512)(128)(4,1)S(1)} %get-tuple-element.237), kind=kOutput, calls=%fused_computation.5.clone.1 | convolution fusion | flops 1077936128 | bytes 29360256 | tf_op jit(solution)/shard_map/while/body/trc,tch->trh/dot_general | solution.py:31
  60.2 17.7 %copy.29 = f32[128,128,256]{0,2,1:T(8,128)} copy(f32[128,128,256]{1,2,0:T(8,128)} %convolution_bitcast_fusion.4) | data formatting | bytes 33554432 | tf_op jit(solution)/shard_map/while/body/trc,tch->trh/dot_general | solution.py:31
  77.9 11.2 %bitcast_select_fusion.4 = f32[128,32768]{0,1:T(8,128)} fusion(f32[128,128,256]{0,2,1:T(8,128)} %copy.29, pred[128]{0:T(512)(128)(4,1)S(1)} %get-tuple-element.238), kind=kLoop, calls=%fused_computation.4.clone.1 | loop fusion | flops 4194304 | bytes 33554560 | tf_op jit(solution)/shard_map/while/body/jit(_where)/select_n | solution.py:36
  89.1 17.4 %copy.30 = f32[128,32768]{1,0:T(8,128)} copy(f32[128,32768]{0,1:T(8,128)} %bitcast_select_fusion.4) | data formatting | bytes 33554432 | tf_op jit(solution)/shard_map/while/body/jit(_where)/select_n | solution.py:36
  106.6 27.7 %scatter_fusion = f32[32,32768]{1,0:T(8,128)} fusion(f32[32,32768]{1,0:T(8,128)} %get-tuple-element.262, s32[128]{0:T(128)S(1)} %get-tuple-element.235, f32[128,32768]{1,0:T(8,128)} %copy.30), kind=kCustom, calls=%fused_computation.2.clone.1 | custom fusion | flops 4194304 | bytes 50332160 | tf_op jit(solution)/shard_map/while/body/scatter-add | solution.py:37
  134.6 4.9 reshape.116
  142.0 6.6 %all-to-all-start = ((bf16[16,256,256]{2,1,0:T(8,128)(2,1)}), bf16[16,256,256]{2,1,0:T(8,128)(2,1)}, u32[]{:S(2)}, u32[]{:S(2)}) async-start(bf16[16,256,256]{2,1,0:T(8,128)(2,1)} %stack.2), calls=%async_computation | async-start | bytes 4194304 | tf_op jit(solution)/shard_map/all_to_all | solution.py:8
  148.6 118.4 %all-reduce.3.cloned.1.call-done = f32[4096,256]{1,0:T(8,128)} async-done(((f32[4096,256]{1,0:T(8,128)}), f32[4096,256]{1,0:T(8,128)}) %all-reduce.3.cloned.1.call-update) | async-done | bytes 4194320 | tf_op jit(solution)/shard_map/psum | solution.py:62
  267.1 2.6 multiply_convert_fusion
  269.7 6.0 %fusion.13 = (bf16[4096,256]{1,0:T(8,128)(2,1)S(1)}, f32[4096,256]{1,0:T(8,128)}) fusion(bf16[16,256,256]{2,1,0:T(8,128)(2,1)} %all-to-all-done, bf16[4096,256]{1,0:T(8,128)(2,1)S(1)} %multiply_convert_fusion, bf16[256,256]{1,0:T(8,128)(2,1)S(1)} %copy-done), kind=kOutput, calls=%fused_computation.35 | convolution fusion | flops 547356672 | bytes 10616832 | tf_op jit(solution)/shard_map/dot_general | solution.py:64
  275.7 2.0 fusion.12
  277.8 92.8 %while.21 = (s32[]{:T(128)}, f32[16,32768]{1,0:T(8,128)S(1)}, s32[]{:T(128)}, s32[128]{0:T(128)S(1)}, s32[]{:T(128)}, /*index=5*/s32[128]{0:T(128)S(1)}, bf16[32...) while((s32[]{:T(128)}, f32[16,32768]{1,0:T(8,128)S(1)}, s32[]{:T(128)}, ...), condition=%wide.region_6.7_spmd, body=%wide.region_4.6_spmd.sunk | while | flops 1086327552 | bytes 197141120 | solution.py:40
  278.1 8.2 %gather_fusion.1 = bf16[128,128,256]{2,1,0:T(8,128)(2,1)} fusion(bf16[32,128,256]{2,1,0:T(8,128)(2,1)} %get-tuple-element.307, s32[1024]{0:T(1024)S(1)} %pad_clamp_fusion.5), kind=kCustom, calls=%fused_computation.1.clone.1 | custom fusion | bytes 16777728 | tf_op jit(solution)/shard_map/while/body/jit(_take)/gather | solution.py:25
  286.9 12.8 %convolution_bitcast_fusion.5 = f32[128,128,256]{1,2,0:T(8,128)} fusion(bf16[128,128,128]{2,1,0:T(8,128)(2,1)} %get-tuple-element.308, bf16[128,128,256]{2,1,0:T(8,128)(2,1)} %gather_fusion.1, pred[128]{0:T(512)(128)(4,1)S(1)} %get-tuple-element.249), kind=kOutput, calls=%fused_computation.19.clone.1 | convolution fusion | flops 1077936128 | bytes 29360256 | tf_op jit(solution)/shard_map/while/body/trc,trh->tch/dot_general | solution.py:27
  299.7 17.7 %copy.31 = f32[128,128,256]{0,2,1:T(8,128)} copy(f32[128,128,256]{1,2,0:T(8,128)} %convolution_bitcast_fusion.5) | data formatting | bytes 33554432 | tf_op jit(solution)/shard_map/while/body/trc,trh->tch/dot_general | solution.py:27
  317.4 11.3 %bitcast_select_fusion.5 = f32[128,32768]{0,1:T(8,128)} fusion(f32[128,128,256]{0,2,1:T(8,128)} %copy.31, pred[128]{0:T(512)(128)(4,1)S(1)} %get-tuple-element.250), kind=kLoop, calls=%fused_computation.18.clone.1 | loop fusion | flops 4194304 | bytes 33554560 | tf_op jit(solution)/shard_map/while/body/jit(_where)/select_n | solution.py:36
  328.7 17.4 %copy.32 = f32[128,32768]{1,0:T(8,128)} copy(f32[128,32768]{0,1:T(8,128)} %bitcast_select_fusion.5) | data formatting | bytes 33554432 | tf_op jit(solution)/shard_map/while/body/jit(_where)/select_n | solution.py:36
  346.1 24.3 %scatter_fusion.1 = f32[16,32768]{1,0:T(8,128)S(1)} fusion(f32[16,32768]{1,0:T(8,128)S(1)} %get-tuple-element.292, s32[128]{0:T(128)S(1)} %get-tuple-element.247, f32[128,32768]{1,0:T(8,128)} %copy.32), kind=kCustom, calls=%fused_computation.3.clone.1 | custom fusion | flops 4194304 | bytes 50332160 | tf_op jit(solution)/shard_map/while/body/scatter-add | solution.py:37
  375.9 27.6 %reduce-scatter.2.cloned.1.call-done = f32[256,256]{1,0:T(8,128)} async-done(((f32[2048,256]{1,0:T(8,128)}), f32[256,256]{1,0:T(8,128)}) %reduce-scatter.2.cloned.1.call-update) | async-done | bytes 262160 | tf_op jit(solution)/shard_map/reduce_scatter | solution.py:80
  405.2 148.4 %all-reduce.5.cloned.1.call-done = f32[256,256]{1,0:T(8,128)} async-done(((f32[256,256]{1,0:T(8,128)}), f32[256,256]{1,0:T(8,128)}) %all-reduce.5.cloned.1.call-update) | async-done | bytes 262160 | tf_op jit(solution)/shard_map/psum | solution.py:76
  (44 shorter events, 16.3 us)
Async XLA Ops:
  7.2 262.5 %copy-start = (bf16[256,256]{1,0:T(8,128)(2,1)S(1)}, bf16[256,256]{1,0:T(8,128)(2,1)}, u32[]{:S(2)}) copy-start(bf16[256,256]{1,0:T(8,128)(2,1)} %param.18) | copy-start | bytes 393220
  7.2 30.2 %all-gather.2.cloned.1.call-start = ((), (), s32[]{:S(2)}) async-start(), calls=%async_computation.2 | async-start | bytes 1179648 | tf_op jit(solution)/shard_map/all_gather | solution.py:54
  8.0 0.5 copy-start.7
  10.2 256.8 %all-reduce.3.cloned.1.call-start = ((), (), s32[]{:S(2)}) async-start(), calls=%async_computation.3 | async-start | bytes 8388608 | tf_op jit(solution)/shard_map/psum | solution.py:62
  37.4 2.3 copy-start.2
  139.5 0.9 copy-start.5
  140.4 8.2 %copy-start.6 = (s32[4096]{0:T(1024)S(1)}, s32[4096]{0:T(1024)}, u32[]{:S(2)}) copy-start(s32[4096]{0:T(1024)} %param.14) | copy-start | bytes 49156
  142.0 127.7 %all-to-all-start = ((bf16[16,256,256]{2,1,0:T(8,128)(2,1)}), bf16[16,256,256]{2,1,0:T(8,128)(2,1)}, u32[]{:S(2)}, u32[]{:S(2)}) async-start(bf16[16,256,256]{2,1,0:T(8,128)(2,1)} %stack.2), calls=%async_computation | async-start | bytes 4194304 | tf_op jit(solution)/shard_map/all_to_all | solution.py:8
  148.5 254.9 %reduce-scatter.2.cloned.1.call-start = ((), (), s32[]{:S(2)}) async-start(), calls=%async_computation.4 | async-start | bytes 2359296 | tf_op jit(solution)/shard_map/reduce_scatter | solution.py:80
  269.7 6.0 %copy-start.3 = (bf16[4096,256]{1,0:T(8,128)(2,1)}, bf16[4096,256]{1,0:T(8,128)(2,1)S(1)}, u32[]{:S(2)}) copy-start(bf16[4096,256]{1,0:T(8,128)(2,1)S(1)} %multiply_convert_fusion) | copy-start | bytes 6291460
  275.7 2.0 copy-start.4
  370.7 32.8 %copy-start.8 = (f32[256]{0:T(256)S(1)}, f32[256]{0:T(256)}, u32[]{:S(2)}) copy-start(f32[256]{0:T(256)} %copy-done.7) | copy-start | bytes 3076
  370.7 184.6 %copy-start.1 = (bf16[256,256]{1,0:T(8,128)(2,1)S(1)}, bf16[256,256]{1,0:T(8,128)(2,1)}, u32[]{:S(2)}) copy-start(bf16[256,256]{1,0:T(8,128)(2,1)} %param.18) | copy-start | bytes 393220
  372.2 181.4 %all-reduce.5.cloned.1.call-start = ((), (), s32[]{:S(2)}) async-start(), calls=%async_computation.5 | async-start | bytes 524288 | tf_op jit(solution)/shard_map/psum | solution.py:76
Sparse Core Ops, SparseCore 0:
  10.3 27.0 all-gather.1
  139.7 127.3 all-reduce.2
  372.3 31.0 reduce-scatter.1
  408.6 144.8 all-reduce.4
